TPU v7x, 32 devices: a whole 2x2x4 slice. The times are simulated.
32 devices in a mesh: section: 2 (over core), expert: 8 (over z, x), dp: 2 (over y).
Axes of the slice: x: 2, y: 2, z: 4, core: 2. Of those that a mesh axis runs over, the one named last changes fastest.
Arguments:
- tokens: bfloat16 [2, 16, 65, 768], P(None, ('expert', 'dp')), may hold values from -6 to 6
- cotangent: bfloat16 [2, 16, 65, 768], P(None, ('expert', 'dp')), may hold values from -6 to 6
- routes: int32 [2, 2, 16, 65, 2], P('section', None, ('expert', 'dp')), may hold values from 0 to 7, all different within a row; in each aligned block of 65 rows (0 to 64, 65 to 129, ..., all dimensions but the last counted through in order) at most 25 rows name the same one
- norm1_gain: bfloat16 [2, 768], P('section', 'dp'), may hold values from 0.099609375 to 1.8984375
- qkv_weight: bfloat16 [2, 768, 2304], P('section', 'dp'), may hold values from -1 to 1
- out_weight: bfloat16 [2, 768, 768], P('section', 'dp'), may hold values from -1.25 to 1.25
- norm2_gain: bfloat16 [2, 768], P('section', 'dp'), may hold values from 0.099609375 to 1.8984375
- router_weight: bfloat16 [2, 768, 8], P('section', 'dp'), may hold values from -1 to 1
- expert_in: bfloat16 [2, 8, 768, 3072], P('section', 'expert', None, 'dp'), may hold values from -0.21875 to 0.21875
- expert_out: bfloat16 [2, 8, 3072, 768], P('section', 'expert', 'dp'), may hold values from -0.875 to 0.875
Outputs:
- boundary: float32 [2, 2, 16, 65, 768], P('section', None, ('expert', 'dp'))
- grad_norm1: float32 [2, 768], P('section', 'dp')
- grad_qkv: float32 [2, 768, 2304], P('section', 'dp')
- grad_proj: float32 [2, 768, 768], P('section', 'dp')
- grad_norm2: float32 [2, 768], P('section', 'dp')
- grad_router: float32 [2, 768, 8], P('section', 'dp')
- grad_expert_in: float32 [2, 8, 768, 3072], P('section', 'expert', None, 'dp')
- grad_expert_out: float32 [2, 8, 3072, 768], P('section', 'expert', 'dp')
Inputs may be any that keep to these rules, and one draw needn't show every extreme that they name: `routes`: in every aligned block of 65 rows (the images of one device in one micro-batch of one section) no expert is named by more than 25 rows, a bound that some block reaches; the two experts of a token differ.
All inputs are finite; a program needn't handle non-finite values.
Results may differ from a plain program's by a relative error of at most 0.03.
Values may be sent and summed in bfloat16 or wider, within the bound.
No kernel may reach another device: no remote copies, remote signals or barrier semaphores. Data moves between devices by JAX's collectives and lax.ppermute only.
A program may use at most 192 MiB of HBM per device.

v0:
```python
import jax
import jax.numpy as jnp
from jax import lax
from jax.sharding import PartitionSpec as P

HEAD = 64
EPSILON = 1e-06


def passed_along(value, axis, steps):
    count = lax.axis_size(axis)
    leading, last = (max(0, -steps), min(count, count - steps))
    return lax.ppermute(value, axis, [(source, source + steps) for source in range(leading, last)])


def shortened(x):
    return jax.tree.map(lambda a: a.astype(jnp.bfloat16) if a.dtype == jnp.float32 else a, x)


def norm_forward(values, norm_gain):
    center = values - jnp.mean(values, axis=-1, keepdims=True)
    inverse = lax.rsqrt(jnp.mean(center * center, axis=-1, keepdims=True) + EPSILON)
    normed = center * inverse
    return (normed * norm_gain, normed, inverse)


def norm_backward(grad_out, normed, inverse, norm_gain):
    grad_hat = grad_out * norm_gain
    grad_gain = jnp.sum(grad_out * normed, axis=0)
    grad_in = inverse * (
        grad_hat
        - jnp.mean(grad_hat, axis=-1, keepdims=True)
        - normed * jnp.mean(grad_hat * normed, axis=-1, keepdims=True)
    )
    return (grad_in, grad_gain)


def gelu_slope(pre_act):
    return (
        0.5 * (1.0 + lax.erf(pre_act * 0.7071067811865476))
        + pre_act * jnp.exp(-0.5 * pre_act * pre_act) * 0.3989422804014327
    )


def attention_forward(a_norm, weight_qkv, images):
    heads = weight_qkv.shape[1] // (3 * HEAD)
    qkv_rows = jnp.dot(a_norm, weight_qkv, preferred_element_type=jnp.float32).astype(jnp.bfloat16)
    shaped = qkv_rows.reshape(images, -1, 3, heads, HEAD)
    scores = jnp.einsum(
        "ishd,ithd->ihst", shaped[:, :, 0], shaped[:, :, 1], preferred_element_type=jnp.float32
    ) * HEAD ** (-0.5)
    row_max = jnp.max(scores, axis=-1, keepdims=True)
    log_total = row_max + jnp.log(jnp.sum(jnp.exp(scores - row_max), axis=-1, keepdims=True))
    attn_probs = jnp.exp(scores - log_total).astype(jnp.bfloat16)
    attended = jnp.einsum(
        "ihst,ithd->ishd", attn_probs, shaped[:, :, 2], preferred_element_type=jnp.float32
    )
    attended = attended.astype(jnp.bfloat16).reshape(a_norm.shape[0], heads * HEAD)
    return (qkv_rows, log_total, attended)


def attention_backward(grad_attended, qkv_rows, log_total, images):
    heads = qkv_rows.shape[1] // (3 * HEAD)
    shaped = qkv_rows.reshape(images, -1, 3, heads, HEAD)
    query_part = shaped[:, :, 0]
    key_part = shaped[:, :, 1]
    value_part = shaped[:, :, 2]
    score_scale = HEAD ** (-0.5)
    scores = (
        jnp.einsum("ishd,ithd->ihst", query_part, key_part, preferred_element_type=jnp.float32)
        * score_scale
    )
    attn_probs = jnp.exp(scores - log_total)
    probs_low = attn_probs.astype(jnp.bfloat16)
    grad_heads = grad_attended.reshape(images, -1, heads, HEAD)
    grad_value = jnp.einsum(
        "ihst,ishd->ithd", probs_low, grad_heads, preferred_element_type=jnp.float32
    )
    grad_probs = jnp.einsum(
        "ishd,ithd->ihst", grad_heads, value_part, preferred_element_type=jnp.float32
    )
    grad_scores = (
        attn_probs
        * (grad_probs - jnp.sum(attn_probs * grad_probs, axis=-1, keepdims=True))
        * score_scale
    )
    grad_scores = grad_scores.astype(jnp.bfloat16)
    grad_query = jnp.einsum(
        "ihst,ithd->ishd", grad_scores, key_part, preferred_element_type=jnp.float32
    )
    grad_key = jnp.einsum(
        "ihst,ishd->ithd", grad_scores, query_part, preferred_element_type=jnp.float32
    )
    stacked = jnp.stack([grad_query, grad_key, grad_value], axis=2)
    return stacked.astype(jnp.bfloat16).reshape(qkv_rows.shape[0], 3 * heads * HEAD)


def shards(
    tokens,
    cotangent,
    routes,
    norm1_gain,
    qkv_weight,
    out_weight,
    norm2_gain,
    router_weight,
    expert_in,
    expert_out,
):
    gathered = (
        lax.all_gather(norm1_gain, "dp", axis=1, tiled=True),
        lax.all_gather(qkv_weight, "dp", axis=1, tiled=True),
        lax.all_gather(out_weight, "dp", axis=1, tiled=True),
        lax.all_gather(norm2_gain, "dp", axis=1, tiled=True),
        lax.all_gather(router_weight, "dp", axis=1, tiled=True),
    )
    norm_one, weight_qkv, weight_proj, norm_two, weight_router = [member[0] for member in gathered]
    gain_one = norm_one.astype(jnp.float32)
    gain_two = norm_two.astype(jnp.float32)
    weight_in = expert_in[0, 0]
    weight_back = expert_out[0, 0]
    section_id = lax.axis_index("section")
    micro_count = tokens.shape[0]
    images = tokens.shape[1]
    seq_len = tokens.shape[2]
    model_width = tokens.shape[3]
    token_count = images * seq_len
    experts = weight_router.shape[1]
    capacity = max(2, (3 * token_count + experts - 1) // experts)
    pair_size = lax.axis_size("dp")
    section_routes = routes[0]

    def owner_trip(send_rows, work):
        spread = jnp.broadcast_to(
            send_rows.reshape(experts, 1, capacity, model_width),
            (experts, pair_size, capacity, model_width),
        )
        spread = spread.reshape(experts * pair_size, capacity, model_width)
        group_rows = lax.all_to_all(
            spread, ("expert", "dp"), split_axis=0, concat_axis=0, tiled=True
        )
        result, extra_out = work(group_rows)
        returned = lax.all_to_all(
            result.astype(jnp.bfloat16), ("expert", "dp"), split_axis=0, concat_axis=0, tiled=True
        ).astype(result.dtype)
        slot_total = jnp.sum(returned.reshape(experts, pair_size, capacity, model_width), axis=1)
        slot_total = slot_total.reshape(experts * capacity, model_width)
        return (slot_total, group_rows, extra_out)

    def expert_forward_work(group_rows):
        pre_act = jnp.einsum(
            "ksd,df->ksf", group_rows, weight_in, preferred_element_type=jnp.float32
        )
        hidden = jax.nn.gelu(pre_act, approximate=False).astype(jnp.bfloat16)
        return (
            jnp.einsum("ksf,fd->ksd", hidden, weight_back, preferred_element_type=jnp.float32),
            None,
        )

    def layer_backward(grad_in, kept_state):
        (
            a_norm,
            hat_one,
            inv_one,
            qkv_rows,
            log_total,
            attended,
            hat_two,
            inv_two,
            b_norm,
            router,
            pair_ids,
            gate_vals,
            slot_place,
            dispatch,
            group_rows,
            expert_rows,
        ) = kept_state
        grad_gate = jnp.sum(grad_in[:, None, :] * expert_rows.astype(jnp.float32), axis=-1)
        grad_rows = (
            (gate_vals[:, :, None] * grad_in[:, None, :])
            .astype(jnp.bfloat16)
            .reshape(-1, model_width)
        )
        send_grads = jnp.dot(dispatch, grad_rows, preferred_element_type=jnp.float32).astype(
            jnp.bfloat16
        )

        def expert_backward_work(group_grads):
            pre_act = jnp.einsum(
                "ksd,df->ksf", group_rows, weight_in, preferred_element_type=jnp.float32
            )
            hidden = jax.nn.gelu(pre_act, approximate=False).astype(jnp.bfloat16)
            grad_weight_back = jnp.einsum(
                "ksf,ksd->fd", hidden, group_grads, preferred_element_type=jnp.float32
            )
            grad_hidden = jnp.einsum(
                "ksd,fd->ksf", group_grads, weight_back, preferred_element_type=jnp.float32
            )
            grad_pre = (grad_hidden * gelu_slope(pre_act)).astype(jnp.bfloat16)
            grad_weight_in = jnp.einsum(
                "ksd,ksf->df", group_rows, grad_pre, preferred_element_type=jnp.float32
            )
            grad_slot_rows = jnp.einsum(
                "ksf,df->ksd", grad_pre, weight_in, preferred_element_type=jnp.float32
            )
            return (grad_slot_rows, (grad_weight_in, grad_weight_back))

        grad_total, unused, expert_terms = owner_trip(send_grads, expert_backward_work)
        grad_b_expert = jnp.sum(
            jnp.take(grad_total, slot_place, axis=0).reshape(token_count, 2, model_width), axis=1
        )
        choose = (
            pair_ids[:, :, None] == jnp.arange(experts, dtype=jnp.int32)[None, None, :]
        ).astype(jnp.float32)
        grad_prob = jnp.sum(choose * grad_gate[:, :, None], axis=1)
        grad_logit = router * (grad_prob - jnp.sum(router * grad_prob, axis=-1, keepdims=True))
        grad_logit = grad_logit.astype(jnp.bfloat16)
        grad_router_w = jnp.dot(b_norm.T, grad_logit, preferred_element_type=jnp.float32)
        grad_b = (
            jnp.dot(grad_logit, weight_router.T, preferred_element_type=jnp.float32) + grad_b_expert
        )
        grad_resid_norm, grad_gain_two = norm_backward(grad_b, hat_two, inv_two, gain_two)
        grad_resid = grad_in + grad_resid_norm
        grad_low = grad_resid.astype(jnp.bfloat16)
        grad_proj_w = jnp.dot(attended.T, grad_low, preferred_element_type=jnp.float32)
        grad_attended = jnp.dot(grad_low, weight_proj.T, preferred_element_type=jnp.float32).astype(
            jnp.bfloat16
        )
        grad_qkv_rows = attention_backward(grad_attended, qkv_rows, log_total, images)
        grad_qkv_w = jnp.dot(a_norm.T, grad_qkv_rows, preferred_element_type=jnp.float32)
        grad_a = jnp.dot(grad_qkv_rows, weight_qkv.T, preferred_element_type=jnp.float32)
        grad_token_norm, grad_gain_one = norm_backward(grad_a, hat_one, inv_one, gain_one)
        grad_tokens = grad_resid + grad_token_norm
        dense_terms = (grad_gain_one, grad_qkv_w, grad_proj_w, grad_gain_two, grad_router_w)
        return (grad_tokens, dense_terms, expert_terms)

    zero_rows = jnp.zeros((images, seq_len, model_width), jnp.bfloat16)
    forward_state = []
    forward_out = []
    passed = zero_rows
    for tick_index in range(micro_count + 1):
        if tick_index > 0:
            passed = passed_along(section_output, "section", 1)
        layer_in = jnp.where(section_id == 0, tokens[min(tick_index, micro_count - 1)], passed)
        micro_id = jnp.clip(tick_index - section_id, 0, micro_count - 1)
        route_ids = lax.dynamic_index_in_dim(section_routes, micro_id, 0, keepdims=False)
        token_rows = layer_in.reshape(token_count, model_width).astype(jnp.float32)
        a_full, layer_hat_one, layer_inv_one = norm_forward(token_rows, gain_one)
        layer_a_norm = a_full.astype(jnp.bfloat16)
        layer_qkv_rows, layer_log_total, layer_attended = attention_forward(
            layer_a_norm, weight_qkv, images
        )
        residual = token_rows + jnp.dot(
            layer_attended, weight_proj, preferred_element_type=jnp.float32
        )
        b_full, layer_hat_two, layer_inv_two = norm_forward(residual, gain_two)
        layer_b_norm = b_full.astype(jnp.bfloat16)
        logits = jnp.dot(layer_b_norm, weight_router, preferred_element_type=jnp.float32)
        layer_router = jax.nn.softmax(logits, axis=-1)
        layer_pair_ids = route_ids.reshape(token_count, 2)
        layer_gate_vals = jnp.take_along_axis(layer_router, layer_pair_ids, axis=1)
        flat_routes = route_ids.reshape(-1)
        onehot = (flat_routes[:, None] == jnp.arange(experts, dtype=jnp.int32)[None, :]).astype(
            jnp.int32
        )
        slot_pos = jnp.sum(onehot * (jnp.cumsum(onehot, axis=0) - 1), axis=1)
        slot_slot_place = flat_routes * capacity + slot_pos
        slot_dispatch = (
            slot_slot_place[None, :] == jnp.arange(experts * capacity, dtype=jnp.int32)[:, None]
        ).astype(jnp.bfloat16)
        layer_send_rows = jnp.dot(
            slot_dispatch, jnp.repeat(layer_b_norm, 2, axis=0), preferred_element_type=jnp.float32
        ).astype(jnp.bfloat16)
        layer_slot_total, layer_group_rows, layer_unused = owner_trip(
            layer_send_rows, expert_forward_work
        )
        slot_out = layer_slot_total.astype(jnp.bfloat16)
        layer_expert_rows = jnp.take(slot_out, slot_slot_place, axis=0).reshape(
            token_count, 2, model_width
        )
        layer_out = residual + jnp.sum(
            layer_gate_vals[:, :, None] * layer_expert_rows.astype(jnp.float32), axis=1
        )
        layer_kept_state = (
            layer_a_norm,
            layer_hat_one,
            layer_inv_one,
            layer_qkv_rows,
            layer_log_total,
            layer_attended,
            layer_hat_two,
            layer_inv_two,
            layer_b_norm,
            layer_router,
            layer_pair_ids,
            layer_gate_vals,
            slot_slot_place,
            slot_dispatch,
            layer_group_rows,
            layer_expert_rows,
        )
        layer_out, kept_state = (layer_out, layer_kept_state)
        section_output = layer_out.astype(jnp.bfloat16).reshape(images, seq_len, model_width)
        forward_state.append(kept_state)
        forward_out.append(layer_out)
    dense_sum = None
    expert_sum = None
    grad_inputs = []
    grad_carry = zero_rows
    for tick_index in range(micro_count + 1):
        kept_state = forward_state[micro_count - tick_index]
        own_cot = cotangent[micro_count - 1 - tick_index] if tick_index < micro_count else zero_rows
        passed_grad = passed_along(grad_carry, "section", -1) if tick_index > 0 else zero_rows
        grad_in = (
            jnp.where(section_id == 1, own_cot, passed_grad)
            .reshape(token_count, model_width)
            .astype(jnp.float32)
        )
        grad_tokens, dense_terms, expert_terms = layer_backward(grad_in, kept_state)
        grad_carry = grad_tokens.astype(jnp.bfloat16).reshape(images, seq_len, model_width)
        grad_inputs.append(grad_tokens)
        if dense_sum is None:
            dense_sum = dense_terms
            expert_sum = expert_terms
        else:
            dense_sum = tuple(
                (
                    first_term + second_term
                    for first_term, second_term in zip(dense_sum, dense_terms)
                )
            )
            expert_sum = tuple(
                (
                    first_term + second_term
                    for first_term, second_term in zip(expert_sum, expert_terms)
                )
            )
    end_values = []
    for micro_index in range(micro_count):
        picked = jnp.where(
            section_id == 0, grad_inputs[micro_count - micro_index], forward_out[micro_index + 1]
        )
        end_values.append(picked.reshape(images, seq_len, model_width))
    boundary = jnp.stack(end_values)[None]
    shares = jax.tree.map(
        lambda part: part.astype(jnp.float32),
        lax.psum_scatter(shortened(dense_sum), "dp", scatter_dimension=0, tiled=True),
    )
    full_sums = jax.tree.map(
        lambda part: part.astype(jnp.float32), lax.psum(shortened(shares), "expert")
    )
    return (
        boundary,
        full_sums[0][None],
        full_sums[1][None],
        full_sums[2][None],
        full_sums[3][None],
        full_sums[4][None],
        expert_sum[0][None, None],
        expert_sum[1][None, None],
    )


def solution(mesh):
    in_specs = (
        P(None, ("expert", "dp"), None, None),
        P(None, ("expert", "dp"), None, None),
        P("section", None, ("expert", "dp"), None, None),
        P("section", "dp"),
        P("section", "dp", None),
        P("section", "dp", None),
        P("section", "dp"),
        P("section", "dp", None),
        P("section", "expert", None, "dp"),
        P("section", "expert", "dp", None),
    )
    out_specs = (
        P("section", None, ("expert", "dp"), None, None),
        P("section", "dp"),
        P("section", "dp", None),
        P("section", "dp", None),
        P("section", "dp"),
        P("section", "dp", None),
        P("section", "expert", None, "dp"),
        P("section", "expert", "dp", None),
    )
    return jax.shard_map(shards, mesh=mesh, in_specs=in_specs, out_specs=out_specs, check_vma=False)
```

profile of v0, /device:TPU:0, one launch (start us, length us, event | category | flops | bytes accessed | tf_op | source)
XLA Modules:
  0.0 877.7 jit_solution(11960009164507809311)
XLA Ops:
  8.7 5.5 all_gather.15
  14.2 4.5 all_gather.18
  23.4 38.3 %all-gather.3.cloned.1.call-done = bf16[1,768,2304]{2,1,0:T(8,128)(2,1)} async-done(((bf16[1,384,2304]{2,1,0:T(8,128)(2,1)}), bf16[1,768,2304]{2,1,0:T(8,128)(2,1)}) %all-gather.3.cloned.1.call-update) | async-done | bytes 3538960 | tf_op jit(solution)/shard_map/all_gather | solution.py:112
  61.6 2.8 fusion.17
  68.2 17.7 %all-gather.5.cloned.1.call-done = bf16[1,768,768]{2,1,0:T(8,128)(2,1)} async-done(((bf16[1,384,768]{2,1,0:T(8,128)(2,1)}), bf16[1,768,768]{2,1,0:T(8,128)(2,1)}) %all-gather.5.cloned.1.call-update) | async-done | bytes 1179664 | tf_op jit(solution)/shard_map/all_gather | solution.py:113
  93.1 5.7 all-to-all-start
  101.4 17.0 %all-to-all-done = bf16[16,25,768]{2,1,0:T(8,128)(2,1)} async-done(((bf16[16,25,768]{2,1,0:T(8,128)(2,1)}), bf16[16,25,768]{2,1,0:T(8,128)(2,1)}, u32[]{:S(2)}, u32[]{:S(2)}) %all-to-all-start) | async-done | bytes 614432 | tf_op jit(solution)/shard_map/all_to_all | solution.py:139
  118.4 3.1 fusion.92
  123.2 7.0 fusion.28
  133.6 5.0 all-to-all-start.1
  139.0 4.9 all_gather.19
  147.9 9.4 %all-to-all-done.1 = bf16[16,25,768]{2,1,0:T(8,128)(2,1)} async-done(((bf16[16,25,768]{2,1,0:T(8,128)(2,1)}), bf16[16,25,768]{2,1,0:T(8,128)(2,1)}, u32[]{:S(2)}, u32[]{:S(2)}) %all-to-all-start.1) | async-done | bytes 614432 | tf_op jit(solution)/shard_map/all_to_all | solution.py:143
  169.5 3.6 fusion.20
  188.9 26.6 %all_to_all.60 = bf16[16,25,768]{2,1,0:T(8,128)(2,1)S(1)} all-to-all(bf16[16,25,768]{2,1,0:T(8,128)(2,1)S(1)} %bitcast.575), channel_id=1, replica_groups=mesh['section'=2,'expert'=8,'dp'=2] {'expert','dp'}, dimensions={0} | all-to-all | bytes 1228800 | tf_op jit(solution)/shard_map/all_to_all | solution.py:139
  219.1 7.0 fusion.31
  229.5 4.5 all-to-all-start.3
  243.1 9.4 %all-to-all-done.3 = bf16[16,25,768]{2,1,0:T(8,128)(2,1)} async-done(((bf16[16,25,768]{2,1,0:T(8,128)(2,1)}), bf16[16,25,768]{2,1,0:T(8,128)(2,1)}, u32[]{:S(2)}, u32[]{:S(2)}) %all-to-all-start.3) | async-done | bytes 614432 | tf_op jit(solution)/shard_map/all_to_all | solution.py:143
  256.5 2.8 gather_fusion.3
  270.8 3.5 fusion.23
  290.1 26.6 %all_to_all.61 = bf16[16,25,768]{2,1,0:T(8,128)(2,1)S(1)} all-to-all(bf16[16,25,768]{2,1,0:T(8,128)(2,1)S(1)} %bitcast.576), channel_id=1, replica_groups=mesh['section'=2,'expert'=8,'dp'=2] {'expert','dp'}, dimensions={0} | all-to-all | bytes 1228800 | tf_op jit(solution)/shard_map/all_to_all | solution.py:139
  320.3 7.0 fusion.34
  330.7 4.5 all-to-all-start.5
  345.3 8.5 all-to-all-done.5
  357.7 2.8 gather_fusion.4
  377.6 24.9 %all_to_all.62 = bf16[16,25,768]{2,1,0:T(8,128)(2,1)S(1)} all-to-all(bf16[16,25,768]{2,1,0:T(8,128)(2,1)S(1)} %bitcast.577), channel_id=1, replica_groups=mesh['section'=2,'expert'=8,'dp'=2] {'expert','dp'}, dimensions={0} | all-to-all | bytes 1228800 | tf_op jit(solution)/shard_map/all_to_all | solution.py:139
  402.5 4.4 fusion.65
  408.1 2.3 fusion.95
  410.4 4.3 all-to-all-start.7
  415.3 17.8 %all-to-all-done.7 = bf16[16,25,768]{2,1,0:T(8,128)(2,1)} async-done(((bf16[16,25,768]{2,1,0:T(8,128)(2,1)}), bf16[16,25,768]{2,1,0:T(8,128)(2,1)}, u32[]{:S(2)}, u32[]{:S(2)}) %all-to-all-start.7) | async-done | bytes 614432 | tf_op jit(solution)/shard_map/all_to_all | solution.py:143
  437.4 2.9 gather_fusion.6
  457.1 2.5 fusion.146
  459.6 2.5 fusion.147
  463.4 4.1 fusion.217
  481.5 26.4 %all_to_all.63 = bf16[16,25,768]{2,1,0:T(8,128)(2,1)S(1)} all-to-all(bf16[16,25,768]{2,1,0:T(8,128)(2,1)S(1)} %bitcast.578), channel_id=1, replica_groups=mesh['section'=2,'expert'=8,'dp'=2] {'expert','dp'}, dimensions={0} | all-to-all | bytes 1228800 | tf_op jit(solution)/shard_map/all_to_all | solution.py:139
  507.9 4.4 fusion.66
  513.8 23.9 %all_to_all.64 = bf16[16,25,768]{2,1,0:T(8,128)(2,1)S(1)} all-to-all(bf16[16,25,768]{2,1,0:T(8,128)(2,1)S(1)} %fusion.98), channel_id=1, replica_groups=mesh['section'=2,'expert'=8,'dp'=2] {'expert','dp'}, dimensions={0} | all-to-all | bytes 1228800 | tf_op jit(solution)/shard_map/all_to_all | solution.py:143
  540.8 2.9 gather_fusion.7
  543.7 2.7 multiply_reduce_fusion.4
  566.8 2.5 fusion.149
  569.3 2.5 fusion.150
  573.2 4.1 fusion.210
  590.5 24.2 %all_to_all.65 = bf16[16,25,768]{2,1,0:T(8,128)(2,1)S(1)} all-to-all(bf16[16,25,768]{2,1,0:T(8,128)(2,1)S(1)} %bitcast.579), channel_id=1, replica_groups=mesh['section'=2,'expert'=8,'dp'=2] {'expert','dp'}, dimensions={0} | all-to-all | bytes 1228800 | tf_op jit(solution)/shard_map/all_to_all | solution.py:139
  614.7 4.4 fusion.67
  622.6 3.7 all-to-all-start.11
  626.5 2.9 fusion.273
  631.3 14.0 %all-to-all-done.11 = bf16[16,25,768]{2,1,0:T(8,128)(2,1)S(1)} async-done(((bf16[16,25,768]{2,1,0:T(8,128)(2,1)}), bf16[16,25,768]{2,1,0:T(8,128)(2,1)S(1)}, u32[]{:S(2)}, u32[]{:S(2)}) %all-to-all-start.11) | async-done | bytes 614432 | tf_op jit(solution)/shard_map/all_to_all | solution.py:143
  647.2 2.8 multiply_reduce_fusion.3
  663.5 3.2 add_convert_fusion.1
  666.9 5.3 fusion.320
  672.3 4.2 fusion.317
  678.6 8.3 add_convert_fusion
  689.9 5.2 fusion.337
  695.1 3.7 fusion.339
  698.8 3.6 fusion.338
  702.5 3.6 fusion.340
  708.0 8.2 fusion.4
  716.3 22.3 %reduce-scatter.6.cloned.1.call-done = bf16[384,2304]{1,0:T(8,128)(2,1)} async-done(((bf16[768,2304]{1,0:T(8,128)(2,1)}), bf16[384,2304]{1,0:T(8,128)(2,1)}) %reduce-scatter.6.cloned.1.call-update) | async-done | bytes 1769488 | tf_op jit(solution)/shard_map/reduce_scatter | solution.py:348
  738.7 8.2 fusion.3
  746.9 2.5 fusion.204
  749.5 4.9 all-reduce.7
  760.3 23.4 %all-reduce.5 = (bf16[1,384]{1,0:T(2,128)(2,1)S(1)}, bf16[1,384]{1,0:T(2,128)(2,1)S(1)}, bf16[1,384,8]{1,2,0:T(8,128)(2,1)S(1)}) all-reduce(bf16[1,384]{1,0:T(2,128)(2,1)S(1)} %broadcast_in_dim.104, bf16[1,384]{1,0:T(2,128)(2,1)S(1)} %broadcast_in_dim.110, ...), channel_id=1, replica_groups=mesh['section'=2,'expert'=8,'dp'=2] {'expert'}, use_global_device_ids=true, to_apply=%region_73.77 | all-reduce | flops 3840 | bytes 15360 | tf_op jit(solution)/shard_map/psum | solution.py:351
  785.4 79.4 %all-reduce.10.cloned.1.call-done = (bf16[1,384,2304]{2,1,0:T(8,128)(2,1)}, bf16[1,384,768]{2,1,0:T(8,128)(2,1)}) async-done(((bf16[1,384,2304]{2,1,0:T(8,128)(2,1)}, bf16[1,384,768]{2,1,0:T(8,128)(2,1)}), (bf16[1,384,2304]{2,1,0:T(8,128)(2,1)}, bf16[1,384,768]{2,1,0:T(8,128)(2,1)})) %all-reduce.10.cloned.1.call-update) | async-done | bytes 2359312 | tf_op jit(solution)/shard_map/psum | solution.py:351
  864.8 2.3 broadcast_in_dim.109
  867.1 3.5 broadcast_in_dim.107
  (572 shorter events, 253.9 us)
Async XLA Ops:
  7.2 111.2 %copy-start = (bf16[1,1,768,1536]{3,2,1,0:T(8,128)(2,1)S(1)}, bf16[1,1,768,1536]{3,2,1,0:T(8,128)(2,1)}, u32[]{:S(2)}) copy-start(bf16[1,1,768,1536]{3,2,1,0:T(8,128)(2,1)} %param.24) | copy-start | bytes 7077892
  7.2 54.5 %all-gather.3.cloned.1.call-start = ((), (), s32[]{:S(2)}) async-start(), calls=%async_computation.15 | async-start | bytes 5308416 | tf_op jit(solution)/shard_map/all_gather | solution.py:112
  7.9 78.0 %all-gather.5.cloned.1.call-start = ((), (), s32[]{:S(2)}) async-start(), calls=%async_computation.16 | async-start | bytes 1769472 | tf_op jit(solution)/shard_map/all_gather | solution.py:113
  20.0 45.5 %copy-start.100 = (s32[1,1,1,65,2]{3,4,2,1,0:T(2,128)}, s32[1,1,1,65,2]{3,4,2,1,0:T(2,128)S(1)}, u32[]{:S(2)}) copy-start(s32[1,1,1,65,2]{3,4,2,1,0:T(2,128)S(1)} %get-tuple-element.81) | copy-start | bytes 1564
  20.0 79.6 %copy-start.99 = (s32[1,1,1,65,2]{3,4,2,1,0:T(2,128)}, s32[1,1,1,65,2]{3,4,2,1,0:T(2,128)S(1)}, u32[]{:S(2)}) copy-start(s32[1,1,1,65,2]{3,4,2,1,0:T(2,128)S(1)} %get-tuple-element.105) | copy-start | bytes 1564
  20.0 127.1 %copy-start.98 = (s32[1,1,1,65,2]{3,4,2,1,0:T(2,128)}, s32[1,1,1,65,2]{3,4,2,1,0:T(2,128)S(1)}, u32[]{:S(2)}) copy-start(s32[1,1,1,65,2]{3,4,2,1,0:T(2,128)S(1)} %get-tuple-element.103) | copy-start | bytes 1564
  21.5 79.9 %copy-start.95 = (s32[130]{0:T(256)}, s32[130]{0:T(256)S(1)}, u32[]{:S(2)}) copy-start(s32[130]{0:T(256)S(1)} %get-tuple-element.95) | copy-start | bytes 1564
  21.6 139.9 %copy-start.129 = (pred[130]{0:T(512)(128)(4,1)}, pred[130]{0:T(512)(128)(4,1)S(1)}, u32[]{:S(2)}) copy-start(pred[130]{0:T(512)(128)(4,1)S(1)} %get-tuple-element.94) | copy-start | bytes 394
  23.0 145.2 %copy-start.40 = (bf16[1,1,65,768]{3,0,2,1:T(2,128)(2,1)}, bf16[1,1,65,768]{3,0,2,1:T(2,128)(2,1)S(1)}, u32[]{:S(2)}) copy-start(bf16[1,1,65,768]{3,0,2,1:T(2,128)(2,1)S(1)} %get-tuple-element.100) | copy-start | bytes 299524
  23.1 62.9 %copy-start.18 = (bf16[1,1,65,768]{3,2,1,0:T(8,128)(2,1)}, bf16[1,1,65,768]{3,2,1,0:T(8,128)(2,1)S(1)}, u32[]{:S(2)}) copy-start(bf16[1,1,65,768]{3,2,1,0:T(8,128)(2,1)S(1)} %get-tuple-element.97) | copy-start | bytes 299524
  23.1 43.9 %copy-start.104 = (f32[65]{0:T(128)}, f32[65]{0:T(128)S(1)}, u32[]{:S(2)}) copy-start(f32[65]{0:T(128)S(1)} %broadcast_multiply_fusion.17) | copy-start | bytes 784
  23.3 44.9 %copy-start.121 = (f32[65]{0:T(128)}, f32[65]{0:T(128)S(1)}, u32[]{:S(2)}) copy-start(f32[65]{0:T(128)S(1)} %add_rsqrt_fusion.5) | copy-start | bytes 784
  23.4 156.2 %copy-start.68 = (f32[768]{0:T(1024)}, f32[768]{0:T(1024)S(1)}, u32[]{:S(2)}) copy-start(f32[768]{0:T(1024)S(1)} %convert_reduce_fusion.6) | copy-start | bytes 9220
  66.9 19.1 %copy-start.9 = (f32[12,65,65]{1,2,0:T(8,128)}, f32[12,65,65]{1,2,0:T(8,128)S(1)}, u32[]{:S(2)}) copy-start(f32[12,65,65]{1,2,0:T(8,128)S(1)} %get-tuple-element.111) | copy-start | bytes 608404
  67.0 26.1 %copy-start.76 = (f32[12,65]{1,0:T(8,128)}, f32[12,65]{1,0:T(8,128)S(1)}, u32[]{:S(2)}) copy-start(f32[12,65]{1,0:T(8,128)S(1)} %log_add_fusion.2) | copy-start | bytes 9364
  68.2 24.9 %copy-start.42 = (bf16[12,64,65]{2,1,0:T(8,128)(2,1)}, bf16[12,64,65]{2,1,0:T(8,128)(2,1)S(1)}, u32[]{:S(2)}) copy-start(bf16[12,64,65]{2,1,0:T(8,128)(2,1)S(1)} %convolution_convert_fusion.17) | copy-start | bytes 299524
  87.7 78.1 %copy-start.8 = (f32[65,768]{1,0:T(8,128)}, f32[65,768]{1,0:T(8,128)S(1)}, u32[]{:S(2)}) copy-start(f32[65,768]{1,0:T(8,128)S(1)} %get-tuple-element.113) | copy-start | bytes 599044
  87.7 11.9 %copy-start.119 = (f32[65]{0:T(128)}, f32[65]{0:T(128)S(1)}, u32[]{:S(2)}) copy-start(f32[65]{0:T(128)S(1)} %broadcast_multiply_fusion.16) | copy-start | bytes 784
  87.9 11.5 %copy-start.130 = (f32[65]{0:T(128)}, f32[65]{0:T(128)S(1)}, u32[]{:S(2)}) copy-start(f32[65]{0:T(128)S(1)} %add_rsqrt_fusion.4) | copy-start | bytes 784
  88.1 56.4 %copy-start.43 = (bf16[65,768]{1,0:T(8,128)(2,1)}, bf16[65,768]{1,0:T(8,128)(2,1)S(1)}, u32[]{:S(2)}) copy-start(bf16[65,768]{1,0:T(8,128)(2,1)S(1)} %multiply_convert_fusion.5) | copy-start | bytes 299524
  93.1 25.3 %all-to-all-start = ((bf16[16,25,768]{2,1,0:T(8,128)(2,1)}), bf16[16,25,768]{2,1,0:T(8,128)(2,1)}, u32[]{:S(2)}, u32[]{:S(2)}) async-start(bf16[16,25,768]{2,1,0:T(8,128)(2,1)} %bitcast.574), calls=%async_computation | async-start | bytes 1572864 | tf_op jit(solution)/shard_map/all_to_all | solution.py:139
  121.5 9.8 %copy-start.136 = (bf16[1,1,1536,768]{3,2,1,0:T(8,128)(2,1)S(1)}, bf16[1,1,1536,768]{3,2,1,0:T(8,128)(2,1)}, u32[]{:S(2)}) copy-start(bf16[1,1,1536,768]{3,2,1,0:T(8,128)(2,1)} %param.25) | copy-start | bytes 7077892
  131.4 7.6 copy-start.124
  133.6 23.7 %all-to-all-start.1 = ((bf16[16,25,768]{2,1,0:T(8,128)(2,1)}), bf16[16,25,768]{2,1,0:T(8,128)(2,1)}, u32[]{:S(2)}, u32[]{:S(2)}) async-start(bf16[16,25,768]{2,1,0:T(8,128)(2,1)} %fusion.104), calls=%async_computation.1 | async-start | bytes 1572864 | tf_op jit(solution)/shard_map/all_to_all | solution.py:143
  138.6 21.9 %copy-start.113 = (s32[1024]{0:T(1024)}, s32[1024]{0:T(1024)S(1)}, u32[]{:S(2)}) copy-start(s32[1024]{0:T(1024)S(1)} %pad_clamp_fusion.2) | copy-start | bytes 12292
  147.9 19.3 %copy-start.131 = (s32[130]{0:T(256)S(1)}, s32[130]{0:T(256)}, u32[]{:S(2)}) copy-start(s32[130]{0:T(256)} %fusion.292) | copy-start | bytes 1564
  147.9 19.3 %copy-start.132 = (s32[130]{0:T(256)S(1)}, s32[130]{0:T(256)}, u32[]{:S(2)}) copy-start(s32[130]{0:T(256)} %fusion.294) | copy-start | bytes 1564
  165.9 2.2 collective-permute-start
  167.8 67.8 %copy-start.96 = (s32[130]{0:T(256)}, s32[130]{0:T(256)S(1)}, u32[]{:S(2)}) copy-start(s32[130]{0:T(256)S(1)} %get-tuple-element.138) | copy-start | bytes 1564
  169.5 8.4 copy-start.3
  217.4 9.8 %copy-start.137 = (bf16[1,1,1536,768]{3,2,1,0:T(8,128)(2,1)S(1)}, bf16[1,1,1536,768]{3,2,1,0:T(8,128)(2,1)}, u32[]{:S(2)}) copy-start(bf16[1,1,1536,768]{3,2,1,0:T(8,128)(2,1)} %param.25) | copy-start | bytes 7077892
  229.5 23.0 %all-to-all-start.3 = ((bf16[16,25,768]{2,1,0:T(8,128)(2,1)}), bf16[16,25,768]{2,1,0:T(8,128)(2,1)}, u32[]{:S(2)}, u32[]{:S(2)}) async-start(bf16[16,25,768]{2,1,0:T(8,128)(2,1)} %fusion.107), calls=%async_computation.3 | async-start | bytes 1572864 | tf_op jit(solution)/shard_map/all_to_all | solution.py:143
  240.2 19.1 %copy-start.128 = (pred[130]{0:T(512)(128)(4,1)S(1)}, pred[130]{0:T(512)(128)(4,1)}, u32[]{:S(2)}) copy-start(pred[130]{0:T(512)(128)(4,1)} %get-tuple-element.137) | copy-start | bytes 394
  266.3 2.2 collective-permute-start.1
  274.4 7.5 copy-start.69
  274.4 10.9 %copy-start.97 = (s32[130]{0:T(256)S(1)}, s32[130]{0:T(256)}, u32[]{:S(2)}) copy-start(s32[130]{0:T(256)} %get-tuple-element.79) | copy-start | bytes 1564
  280.6 38.0 %copy-start.117 = (f32[65]{0:T(128)}, f32[65]{0:T(128)S(1)}, u32[]{:S(2)}) copy-start(f32[65]{0:T(128)S(1)} %broadcast_multiply_fusion.12) | copy-start | bytes 784
  318.7 9.8 %copy-start.138 = (bf16[1,1,1536,768]{3,2,1,0:T(8,128)(2,1)S(1)}, bf16[1,1,1536,768]{3,2,1,0:T(8,128)(2,1)}, u32[]{:S(2)}) copy-start(bf16[1,1,1536,768]{3,2,1,0:T(8,128)(2,1)} %param.25) | copy-start | bytes 7077892
  330.7 23.0 %all-to-all-start.5 = ((bf16[16,25,768]{2,1,0:T(8,128)(2,1)}), bf16[16,25,768]{2,1,0:T(8,128)(2,1)}, u32[]{:S(2)}, u32[]{:S(2)}) async-start(bf16[16,25,768]{2,1,0:T(8,128)(2,1)} %fusion.110), calls=%async_computation.5 | async-start | bytes 1572864 | tf_op jit(solution)/shard_map/all_to_all | solution.py:143
  339.6 25.7 %copy-start.101 = (s32[1,1,1,65,2]{3,4,2,1,0:T(2,128)S(1)}, s32[1,1,1,65,2]{3,4,2,1,0:T(2,128)}, u32[]{:S(2)}) copy-start(s32[1,1,1,65,2]{3,4,2,1,0:T(2,128)} %copy-done.100) | copy-start | bytes 1564
  410.4 22.7 %all-to-all-start.7 = ((bf16[16,25,768]{2,1,0:T(8,128)(2,1)}), bf16[16,25,768]{2,1,0:T(8,128)(2,1)}, u32[]{:S(2)}, u32[]{:S(2)}) async-start(bf16[16,25,768]{2,1,0:T(8,128)(2,1)} %fusion.95), calls=%async_computation.7 | async-start | bytes 1572864 | tf_op jit(solution)/shard_map/all_to_all | solution.py:143
  437.4 8.9 %copy-start.70 = (f32[768]{0:T(1024)S(1)}, f32[768]{0:T(1024)}, u32[]{:S(2)}) copy-start(f32[768]{0:T(1024)} %copy-done.68) | copy-start | bytes 9220
  437.4 8.9 %copy-start.118 = (f32[65]{0:T(128)S(1)}, f32[65]{0:T(128)}, u32[]{:S(2)}) copy-start(f32[65]{0:T(128)} %copy-done.117) | copy-start | bytes 784
  450.1 13.4 %copy-start.88 = (f32[65]{0:T(128)S(1)}, f32[65]{0:T(128)}, u32[]{:S(2)}) copy-start(f32[65]{0:T(128)} %copy-done.87) | copy-start | bytes 784
  468.4 3.5 collective-permute-start.2
  538.7 11.2 %copy-start.75 = (f32[65,8]{0,1:T(8,128)S(1)}, f32[65,8]{0,1:T(8,128)}, u32[]{:S(2)}) copy-start(f32[65,8]{0,1:T(8,128)} %copy-done.74) | copy-start | bytes 6244
  559.8 13.4 %copy-start.85 = (f32[65]{0:T(128)S(1)}, f32[65]{0:T(128)}, u32[]{:S(2)}) copy-start(f32[65]{0:T(128)} %copy-done.84) | copy-start | bytes 784
  578.2 3.5 collective-permute-start.3
  622.6 22.7 %all-to-all-start.11 = ((bf16[16,25,768]{2,1,0:T(8,128)(2,1)}), bf16[16,25,768]{2,1,0:T(8,128)(2,1)S(1)}, u32[]{:S(2)}, u32[]{:S(2)}) async-start(bf16[16,25,768]{2,1,0:T(8,128)(2,1)} %fusion.101), calls=%async_computation.11 | async-start | bytes 1572864 | tf_op jit(solution)/shard_map/all_to_all | solution.py:143
  626.3 89.9 %reduce-scatter.8.cloned.1.call-start = ((), (), s32[]{:S(2)}) async-start(), calls=%async_computation.18 | async-start | bytes 1769472 | tf_op jit(solution)/shard_map/reduce_scatter | solution.py:348
  645.4 8.2 copy-start.73
  647.2 16.3 %copy-start.4 = (f32[768,768]{1,0:T(8,128)S(1)}, f32[768,768]{1,0:T(8,128)}, u32[]{:S(2)}) copy-start(f32[768,768]{1,0:T(8,128)} %fusion.273) | copy-start | bytes 7077892
  666.8 71.8 %reduce-scatter.6.cloned.1.call-start = ((), (), s32[]{:S(2)}) async-start(), calls=%async_computation.17 | async-start | bytes 5308416 | tf_op jit(solution)/shard_map/reduce_scatter | solution.py:348
  678.6 8.4 copy-start.24
  687.0 72.3 %reduce-scatter.10.cloned.1.call-start = ((), (), s32[]{:S(2)}) async-start(), calls=%async_computation.19 | async-start | bytes 294912
  708.0 156.9 %all-reduce.10.cloned.1.call-start = ((), (), s32[]{:S(2)}) async-start(), calls=%async_computation.20 | async-start | bytes 4718592 | tf_op jit(solution)/shard_map/psum | solution.py:351
  738.6 8.3 copy-start.90
  738.6 8.3 copy-start.92
  738.6 8.3 copy-start.94
  738.6 8.3 copy-start.2
  738.6 8.3 copy-start.20
  738.6 8.3 copy-start.25
  738.7 8.3 copy-start.106
  738.7 8.3 copy-start.123
  (96 other events, 280.9 us)
Sparse Core Ops, SparseCore 0:
  9.5 52.0 all-gather.2
  63.2 22.7 all-gather.4
  666.9 21.1 reduce-scatter.7
  690.8 47.7 reduce-scatter.5
  740.6 11.0 reduce-scatter.9
  755.1 109.6 all-reduce.9
where the time goes:
time: 890 us; the launch traced here: 878 us
  waiting for transfers between devices  239 us (27%)
  blocking collectives  196 us (22%)
  matrix products  166 us (19%)
  local copies, waits for them, and re-layouts  131 us (15%)
  other arithmetic  95.5 us (11%)
  starting transfers between devices  33.4 us (4%)
  between operations  17 us (2%)
    all_to_all x5, blocking collectives, owner_trip(): lax.all_to_all(spread, ('expert', 'dp'), split_axis=0, concat_axis=0, til...  129 us
    psum x1, waiting for transfers between devices, shards(): lax.psum(shortened(shares), 'expert')  79.4 us
    all_to_all x5, waiting for transfers between devices, owner_trip(): lax.all_to_all(result.astype(jnp.bfloat16), ('expert', 'dp'), split_axis=...  59 us
    all_gather x1, waiting for transfers between devices, shards(): lax.all_gather(qkv_weight, 'dp', axis=1, tiled=True)  38.3 us
    unnamed x294, local copies, waits for them, and re-layouts  26.3 us
    all_to_all x1, blocking collectives, owner_trip(): lax.all_to_all(result.astype(jnp.bfloat16), ('expert', 'dp'), split_axis=...  23.9 us
    psum x1, blocking collectives, shards(): lax.psum(shortened(shares), 'expert')  23.4 us
    reduce_scatter x2, waiting for transfers between devices, shards(): lax.psum_scatter(shortened(dense_sum), 'dp', scatter_dimension=0, tiled=T...  22.3 us
  transfers between devices with their start and end apart: 16, of which 14 were waited for; matrix products, arithmetic and copies ran while one was open for 12% of the time, Pallas kernels for 0%

commit v1 on v0

--- a/solution.py
+++ b/solution.py
@@ -5,6 +5,17 @@
 
 HEAD = 64
 EPSILON = 1e-06
+
+
+def in_blocks(x, dim, length):
+    before, after = (x.shape[:dim], x.shape[dim + 1 :])
+    return jnp.moveaxis(x.reshape(*before, length, -1, *after), dim, 0)
+
+
+def joined_along(pieces, dim):
+    shape = list(pieces.shape[1:])
+    shape[dim] *= pieces.shape[0]
+    return jnp.moveaxis(pieces, 0, dim).reshape(shape)
 
 
 def passed_along(value, axis, steps):
@@ -136,9 +147,17 @@
             (experts, pair_size, capacity, model_width),
         )
         spread = spread.reshape(experts * pair_size, capacity, model_width)
-        group_rows = lax.all_to_all(
-            spread, ("expert", "dp"), split_axis=0, concat_axis=0, tiled=True
-        )
+        size, position = (lax.axis_size(("expert", "dp")), lax.axis_index(("expert", "dp")))
+        blocks = in_blocks(spread, 0, size)
+        result_2 = blocks
+        for step in range(1, size):
+            target, source_2 = ((position + step) % size, (position - step) % size)
+            sent = lax.dynamic_index_in_dim(blocks, target, 0)
+            partner_block = lax.ppermute(
+                sent, ("expert", "dp"), [(i, (i + step) % size) for i in range(size)]
+            )
+            result_2 = lax.dynamic_update_slice_in_dim(result_2, partner_block, source_2, axis=0)
+        group_rows = joined_along(result_2, 0)
         result, extra_out = work(group_rows)
         returned = lax.all_to_all(
             result.astype(jnp.bfloat16), ("expert", "dp"), split_axis=0, concat_axis=0, tiled=True

time: 890 us -> 1130 us (1.27)
  waiting for transfers between devices: 239 us -> 467 us
  starting transfers between devices: 33.4 us -> 174 us
  blocking collectives: 196 us -> 64.9 us
    ppermute x0 -> x90, waiting for transfers between devices: none -> 272 us  [owner_trip(): lax.ppermute(sent, ('expert', 'dp'), [(i, (i + step) % size) for i in ran...]
    ppermute x0 -> x90, starting transfers between devices: none -> 135 us  [owner_trip(): lax.ppermute(sent, ('expert', 'dp'), [(i, (i + step) % size) for i in ran...]
    all_to_all x5 -> x0, blocking collectives: 129 us -> none  [owner_trip(): lax.all_to_all(spread, ('expert', 'dp'), split_axis=0, concat_axis=0, til...]
    all_to_all x5, waiting for transfers between devices: 59 us -> 30.8 us  [owner_trip(): lax.all_to_all(result.astype(jnp.bfloat16), ('expert', 'dp'), split_axis=...]
    all_to_all x1 -> x0, waiting for transfers between devices: 17 us -> none  [owner_trip(): lax.all_to_all(spread, ('expert', 'dp'), split_axis=0, concat_axis=0, til...]
    all_to_all x5, starting transfers between devices: 22 us -> 33.6 us  [owner_trip(): lax.all_to_all(result.astype(jnp.bfloat16), ('expert', 'dp'), split_axis=...]
    unnamed x294 -> x316, local copies, waits for them, and re-layouts: 26.3 us -> 26.9 us
  transfers between devices with their start and end apart: 16 -> 105, of which waited for: 14 -> 74; matrix products, arithmetic and copies ran while one was open for 12% -> 10% of each run, Pallas kernels for 0% -> 0%
where the time goes in v1:
time: 1130 us; the launch traced here: 1120 us
  waiting for transfers between devices  467 us (41%)
  starting transfers between devices  174 us (15%)
  matrix products  162 us (14%)
  local copies, waits for them, and re-layouts  141 us (12%)
  other arithmetic  94 us (8%)
  blocking collectives  64.9 us (6%)
  between operations  18.3 us (2%)
    ppermute x90, waiting for transfers between devices, owner_trip(): lax.ppermute(sent, ('expert', 'dp'), [(i, (i + step) % size) for i in ran...  272 us
    ppermute x90, starting transfers between devices, owner_trip(): lax.ppermute(sent, ('expert', 'dp'), [(i, (i + step) % size) for i in ran...  135 us
    psum x1, waiting for transfers between devices, shards(): lax.psum(shortened(shares), 'expert')  83.6 us
    all_gather x1, waiting for transfers between devices, shards(): lax.all_gather(qkv_weight, 'dp', axis=1, tiled=True)  35.6 us
    all_to_all x5, starting transfers between devices, owner_trip(): lax.all_to_all(result.astype(jnp.bfloat16), ('expert', 'dp'), split_axis=...  33.6 us
    all_to_all x5, waiting for transfers between devices, owner_trip(): lax.all_to_all(result.astype(jnp.bfloat16), ('expert', 'dp'), split_axis=...  30.8 us
    unnamed x316, local copies, waits for them, and re-layouts  26.9 us
    psum x1, blocking collectives, shards(): lax.psum(shortened(shares), 'expert')  23.5 us
  transfers between devices with their start and end apart: 105, of which 74 were waited for; matrix products, arithmetic and copies ran while one was open for 10% of the time, Pallas kernels for 0%

profile of v1, /device:TPU:0, one launch (start us, length us, event | category | flops | bytes accessed | tf_op | source)
XLA Modules:
  0.0 1121.7 jit_solution(14150184074577540299)
XLA Ops:
  8.8 5.5 all_gather.15
  14.3 4.5 all_gather.18
  26.1 35.6 %all-gather.3.cloned.1.call-done = bf16[1,768,2304]{2,1,0:T(8,128)(2,1)} async-done(((bf16[1,384,2304]{2,1,0:T(8,128)(2,1)}), bf16[1,768,2304]{2,1,0:T(8,128)(2,1)}) %all-gather.3.cloned.1.call-update) | async-done | bytes 3538960 | tf_op jit(solution)/shard_map/all_gather | solution.py:123
  67.9 18.1 %all-gather.5.cloned.1.call-done = bf16[1,768,768]{2,1,0:T(8,128)(2,1)} async-done(((bf16[1,384,768]{2,1,0:T(8,128)(2,1)}), bf16[1,768,768]{2,1,0:T(8,128)(2,1)}) %all-gather.5.cloned.1.call-update) | async-done | bytes 1179664 | tf_op jit(solution)/shard_map/all_gather | solution.py:124
  94.9 5.3 collective-permute-start.14
  104.4 5.0 collective-permute-done.1
  110.3 6.1 collective-permute-done.2
  117.0 5.5 collective-permute-done.3
  124.8 4.7 collective-permute-done.4
  153.6 4.3 collective-permute-start.9
  173.0 7.0 fusion.28
  183.4 7.0 all-to-all-start
  190.7 4.9 all_gather.19
  243.2 6.5 collective-permute-done.17
  249.6 6.8 collective-permute-done.18
  256.4 5.9 collective-permute-done.19
  263.3 5.8 collective-permute-done.20
  270.4 4.8 collective-permute-done.21
  276.7 4.4 collective-permute-done.22
  307.0 7.0 fusion.31
  317.4 7.0 all-to-all-start.1
  383.0 6.5 collective-permute-done.33
  389.5 6.8 collective-permute-done.34
  396.3 5.9 collective-permute-done.35
  403.3 5.7 collective-permute-done.36
  410.1 5.2 collective-permute-done.37
  416.5 5.4 collective-permute-done.38
  447.7 7.0 fusion.34
  458.1 6.7 all-to-all-start.2
  510.3 6.5 collective-permute-done.48
  516.8 7.0 collective-permute-done.49
  523.8 5.9 collective-permute-done.50
  529.9 6.5 collective-permute-done.51
  537.1 5.3 collective-permute-done.52
  543.5 4.7 collective-permute-done.53
  564.7 4.5 collective-permute-start.57
  578.5 6.6 all-to-all-start.3
  585.8 12.3 %all-to-all-done.3 = bf16[16,25,768]{2,1,0:T(8,128)(2,1)} async-done(((bf16[16,25,768]{2,1,0:T(8,128)(2,1)}), bf16[16,25,768]{2,1,0:T(8,128)(2,1)}, u32[]{:S(2)}, u32[]{:S(2)}) %all-to-all-start.3) | async-done | bytes 614432 | tf_op jit(solution)/shard_map/all_to_all | solution.py:162
  655.2 6.6 collective-permute-done.64
  661.8 6.8 collective-permute-done.65
  668.5 5.9 collective-permute-done.66
  674.7 6.5 collective-permute-done.67
  681.5 5.6 collective-permute-done.68
  688.3 5.0 collective-permute-done.69
  720.4 21.6 %all_to_all.30 = bf16[16,25,768]{2,1,0:T(8,128)(2,1)S(1)} all-to-all(bf16[16,25,768]{2,1,0:T(8,128)(2,1)S(1)} %fusion.98), channel_id=1, replica_groups=mesh['section'=2,'expert'=8,'dp'=2] {'expert','dp'}, dimensions={0} | all-to-all | bytes 1228800 | tf_op jit(solution)/shard_map/all_to_all | solution.py:162
  795.9 5.1 collective-permute-start.93
  803.0 6.8 collective-permute-done.80
  809.8 6.8 collective-permute-done.81
  816.6 5.9 collective-permute-done.82
  822.5 7.1 collective-permute-done.83
  829.7 6.5 collective-permute-done.84
  836.2 5.9 collective-permute-done.85
  842.3 4.7 collective-permute-done.86
  870.6 6.3 all-to-all-start.5
  881.7 8.1 all-to-all-done.5
  911.5 5.3 fusion.320
  923.1 8.1 add_convert_fusion
  934.2 5.2 fusion.337
  951.7 8.1 fusion.4
  959.9 23.1 %reduce-scatter.6.cloned.1.call-done = bf16[384,2304]{1,0:T(8,128)(2,1)} async-done(((bf16[768,2304]{1,0:T(8,128)(2,1)}), bf16[384,2304]{1,0:T(8,128)(2,1)}) %reduce-scatter.6.cloned.1.call-update) | async-done | bytes 1769488 | tf_op jit(solution)/shard_map/reduce_scatter | solution.py:367
  983.0 8.0 fusion.3
  992.5 4.9 all-reduce.7
  999.9 23.5 %all-reduce.5 = (bf16[1,384]{1,0:T(2,128)(2,1)S(1)}, bf16[1,384]{1,0:T(2,128)(2,1)S(1)}, bf16[1,384,8]{1,2,0:T(8,128)(2,1)S(1)}) all-reduce(bf16[1,384]{1,0:T(2,128)(2,1)S(1)} %broadcast_in_dim.104, bf16[1,384]{1,0:T(2,128)(2,1)S(1)} %broadcast_in_dim.110, ...), channel_id=1, replica_groups=mesh['section'=2,'expert'=8,'dp'=2] {'expert'}, use_global_device_ids=true, to_apply=%region_73.77 | all-reduce | flops 3840 | bytes 15360 | tf_op jit(solution)/shard_map/psum | solution.py:370
  1025.2 83.6 %all-reduce.10.cloned.1.call-done = (bf16[1,384,2304]{2,1,0:T(8,128)(2,1)}, bf16[1,384,768]{2,1,0:T(8,128)(2,1)}) async-done(((bf16[1,384,2304]{2,1,0:T(8,128)(2,1)}, bf16[1,384,768]{2,1,0:T(8,128)(2,1)}), (bf16[1,384,2304]{2,1,0:T(8,128)(2,1)}, bf16[1,384,768]{2,1,0:T(8,128)(2,1)})) %all-reduce.10.cloned.1.call-update) | async-done | bytes 2359312 | tf_op jit(solution)/shard_map/psum | solution.py:370
  (863 shorter events, 542.7 us)
Async XLA Ops:
  7.2 54.5 %all-gather.3.cloned.1.call-start = ((), (), s32[]{:S(2)}) async-start(), calls=%async_computation.9 | async-start | bytes 5308416 | tf_op jit(solution)/shard_map/all_gather | solution.py:123
  7.9 78.1 %all-gather.5.cloned.1.call-start = ((), (), s32[]{:S(2)}) async-start(), calls=%async_computation.10 | async-start | bytes 1769472 | tf_op jit(solution)/shard_map/all_gather | solution.py:124
  94.0 8.4 collective-permute-start
  94.9 72.7 %collective-permute-start.14 = (bf16[1,1,25,768]{3,2,1,0:T(8,128)(2,1)S(1)}, bf16[1,1,25,768]{3,2,1,0:T(8,128)(2,1)S(1)}, u32[]{:S(2)}, u32[]{:S(2)}) collective-permute-start(bf16[1,1,25,768]{3,2,1,0:T(8,128)(2,1)S(1)} %get-tuple-element.173), channel_id=1, source_target_pairs={{0,15},{1,0},{2,1},{3,2},{4,3},{5,4},{6,5},{7,6},{8,7},{9,8},{10,9... | collective-permute-start | bytes 115208 | tf_op jit(solution)/shard_map/ppermute | solution.py:156
  100.2 66.7 %collective-permute-start.13 = (bf16[1,1,25,768]{3,2,1,0:T(8,128)(2,1)S(1)}, bf16[1,1,25,768]{3,2,1,0:T(8,128)(2,1)S(1)}, u32[]{:S(2)}, u32[]{:S(2)}) collective-permute-start(bf16[1,1,25,768]{3,2,1,0:T(8,128)(2,1)S(1)} %get-tuple-element.174), channel_id=1, source_target_pairs={{0,14},{1,15},{2,0},{3,1},{4,2},{5,3},{6,4},{7,5},{8,6},{9,7},{10,... | collective-permute-start | bytes 115208 | tf_op jit(solution)/shard_map/ppermute | solution.py:156
  101.8 64.6 %collective-permute-start.12 = (bf16[1,1,25,768]{3,2,1,0:T(8,128)(2,1)S(1)}, bf16[1,1,25,768]{3,2,1,0:T(8,128)(2,1)S(1)}, u32[]{:S(2)}, u32[]{:S(2)}) collective-permute-start(bf16[1,1,25,768]{3,2,1,0:T(8,128)(2,1)S(1)} %get-tuple-element.175), channel_id=1, source_target_pairs={{0,13},{1,14},{2,15},{3,0},{4,1},{5,2},{6,3},{7,4},{8,5},{9,6},{10... | collective-permute-start | bytes 115208 | tf_op jit(solution)/shard_map/ppermute | solution.py:156
  101.8 63.9 %collective-permute-start.11 = (bf16[1,1,25,768]{3,2,1,0:T(8,128)(2,1)S(1)}, bf16[1,1,25,768]{3,2,1,0:T(8,128)(2,1)S(1)}, u32[]{:S(2)}, u32[]{:S(2)}) collective-permute-start(bf16[1,1,25,768]{3,2,1,0:T(8,128)(2,1)S(1)} %get-tuple-element.176), channel_id=1, source_target_pairs={{0,12},{1,13},{2,14},{3,15},{4,0},{5,1},{6,2},{7,3},{8,4},{9,5},{1... | collective-permute-start | bytes 115208 | tf_op jit(solution)/shard_map/ppermute | solution.py:156
  102.4 7.0 collective-permute-start.1
  109.4 7.0 collective-permute-start.2
  122.5 7.0 collective-permute-start.4
  135.6 6.4 collective-permute-start.6
  147.2 6.4 collective-permute-start.8
  183.4 20.0 %all-to-all-start = ((bf16[16,25,768]{2,1,0:T(8,128)(2,1)}), bf16[16,25,768]{2,1,0:T(8,128)(2,1)}, u32[]{:S(2)}, u32[]{:S(2)}) async-start(bf16[16,25,768]{2,1,0:T(8,128)(2,1)} %fusion.104), calls=%async_computation | async-start | bytes 1572864 | tf_op jit(solution)/shard_map/all_to_all | solution.py:162
  234.8 8.0 collective-permute-start.16
  236.3 66.9 %collective-permute-start.30 = (bf16[1,1,25,768]{3,2,1,0:T(8,128)(2,1)S(1)}, bf16[1,1,25,768]{3,2,1,0:T(8,128)(2,1)S(1)}, u32[]{:S(2)}, u32[]{:S(2)}) collective-permute-start(bf16[1,1,25,768]{3,2,1,0:T(8,128)(2,1)S(1)} %get-tuple-element.158), channel_id=1, source_target_pairs={{0,15},{1,0},{2,1},{3,2},{4,3},{5,4},{6,5},{7,6},{8,7},{9,8},{10,9... | collective-permute-start | bytes 115208 | tf_op jit(solution)/shard_map/ppermute | solution.py:156
  240.5 62.7 %collective-permute-start.29 = (bf16[1,1,25,768]{3,2,1,0:T(8,128)(2,1)S(1)}, bf16[1,1,25,768]{3,2,1,0:T(8,128)(2,1)S(1)}, u32[]{:S(2)}, u32[]{:S(2)}) collective-permute-start(bf16[1,1,25,768]{3,2,1,0:T(8,128)(2,1)S(1)} %get-tuple-element.159), channel_id=1, source_target_pairs={{0,14},{1,15},{2,0},{3,1},{4,2},{5,3},{6,4},{7,5},{8,6},{9,7},{10,... | collective-permute-start | bytes 115208 | tf_op jit(solution)/shard_map/ppermute | solution.py:156
  241.2 62.0 %collective-permute-start.28 = (bf16[1,1,25,768]{3,2,1,0:T(8,128)(2,1)S(1)}, bf16[1,1,25,768]{3,2,1,0:T(8,128)(2,1)S(1)}, u32[]{:S(2)}, u32[]{:S(2)}) collective-permute-start(bf16[1,1,25,768]{3,2,1,0:T(8,128)(2,1)S(1)} %get-tuple-element.160), channel_id=1, source_target_pairs={{0,13},{1,14},{2,15},{3,0},{4,1},{5,2},{6,3},{7,4},{8,5},{9,6},{10... | collective-permute-start | bytes 115208 | tf_op jit(solution)/shard_map/ppermute | solution.py:156
  241.2 62.0 %collective-permute-start.27 = (bf16[1,1,25,768]{3,2,1,0:T(8,128)(2,1)S(1)}, bf16[1,1,25,768]{3,2,1,0:T(8,128)(2,1)S(1)}, u32[]{:S(2)}, u32[]{:S(2)}) collective-permute-start(bf16[1,1,25,768]{3,2,1,0:T(8,128)(2,1)S(1)} %get-tuple-element.161), channel_id=1, source_target_pairs={{0,12},{1,13},{2,14},{3,15},{4,0},{5,1},{6,2},{7,3},{8,4},{9,5},{1... | collective-permute-start | bytes 115208 | tf_op jit(solution)/shard_map/ppermute | solution.py:156
  242.8 6.8 collective-permute-start.17
  249.6 6.8 collective-permute-start.18
  262.3 6.8 collective-permute-start.20
  317.4 20.0 %all-to-all-start.1 = ((bf16[16,25,768]{2,1,0:T(8,128)(2,1)}), bf16[16,25,768]{2,1,0:T(8,128)(2,1)}, u32[]{:S(2)}, u32[]{:S(2)}) async-start(bf16[16,25,768]{2,1,0:T(8,128)(2,1)} %fusion.107), calls=%async_computation.1 | async-start | bytes 1572864 | tf_op jit(solution)/shard_map/all_to_all | solution.py:162
  374.7 8.0 collective-permute-start.32
  376.2 67.8 %collective-permute-start.46 = (bf16[1,1,25,768]{3,2,1,0:T(8,128)(2,1)S(1)}, bf16[1,1,25,768]{3,2,1,0:T(8,128)(2,1)S(1)}, u32[]{:S(2)}, u32[]{:S(2)}) collective-permute-start(bf16[1,1,25,768]{3,2,1,0:T(8,128)(2,1)S(1)} %get-tuple-element.143), channel_id=1, source_target_pairs={{0,15},{1,0},{2,1},{3,2},{4,3},{5,4},{6,5},{7,6},{8,7},{9,8},{10,9... | collective-permute-start | bytes 115208 | tf_op jit(solution)/shard_map/ppermute | solution.py:156
  380.4 63.6 %collective-permute-start.45 = (bf16[1,1,25,768]{3,2,1,0:T(8,128)(2,1)S(1)}, bf16[1,1,25,768]{3,2,1,0:T(8,128)(2,1)S(1)}, u32[]{:S(2)}, u32[]{:S(2)}) collective-permute-start(bf16[1,1,25,768]{3,2,1,0:T(8,128)(2,1)S(1)} %get-tuple-element.144), channel_id=1, source_target_pairs={{0,14},{1,15},{2,0},{3,1},{4,2},{5,3},{6,4},{7,5},{8,6},{9,7},{10,... | collective-permute-start | bytes 115208 | tf_op jit(solution)/shard_map/ppermute | solution.py:156
  381.0 62.9 %collective-permute-start.44 = (bf16[1,1,25,768]{3,2,1,0:T(8,128)(2,1)S(1)}, bf16[1,1,25,768]{3,2,1,0:T(8,128)(2,1)S(1)}, u32[]{:S(2)}, u32[]{:S(2)}) collective-permute-start(bf16[1,1,25,768]{3,2,1,0:T(8,128)(2,1)S(1)} %get-tuple-element.145), channel_id=1, source_target_pairs={{0,13},{1,14},{2,15},{3,0},{4,1},{5,2},{6,3},{7,4},{8,5},{9,6},{10... | collective-permute-start | bytes 115208 | tf_op jit(solution)/shard_map/ppermute | solution.py:156
  381.0 62.9 %collective-permute-start.43 = (bf16[1,1,25,768]{3,2,1,0:T(8,128)(2,1)S(1)}, bf16[1,1,25,768]{3,2,1,0:T(8,128)(2,1)S(1)}, u32[]{:S(2)}, u32[]{:S(2)}) collective-permute-start(bf16[1,1,25,768]{3,2,1,0:T(8,128)(2,1)S(1)} %get-tuple-element.146), channel_id=1, source_target_pairs={{0,12},{1,13},{2,14},{3,15},{4,0},{5,1},{6,2},{7,3},{8,4},{9,5},{1... | collective-permute-start | bytes 115208 | tf_op jit(solution)/shard_map/ppermute | solution.py:156
  382.7 6.8 collective-permute-start.33
  389.5 6.8 collective-permute-start.34
  402.2 6.8 collective-permute-start.36
  409.0 6.3 collective-permute-start.37
  415.3 6.6 collective-permute-start.38
  458.1 19.7 %all-to-all-start.2 = ((bf16[16,25,768]{2,1,0:T(8,128)(2,1)}), bf16[16,25,768]{2,1,0:T(8,128)(2,1)}, u32[]{:S(2)}, u32[]{:S(2)}) async-start(bf16[16,25,768]{2,1,0:T(8,128)(2,1)} %fusion.110), calls=%async_computation.2 | async-start | bytes 1572864 | tf_op jit(solution)/shard_map/all_to_all | solution.py:162
  502.0 8.0 collective-permute-start.47
  503.5 67.6 %collective-permute-start.61 = (bf16[1,1,25,768]{3,2,1,0:T(8,128)(2,1)S(1)}, bf16[1,1,25,768]{3,2,1,0:T(8,128)(2,1)S(1)}, u32[]{:S(2)}, u32[]{:S(2)}) collective-permute-start(bf16[1,1,25,768]{3,2,1,0:T(8,128)(2,1)S(1)} %get-tuple-element.128), channel_id=1, source_target_pairs={{0,15},{1,0},{2,1},{3,2},{4,3},{5,4},{6,5},{7,6},{8,7},{9,8},{10,9... | collective-permute-start | bytes 115208 | tf_op jit(solution)/shard_map/ppermute | solution.py:156
  507.6 63.4 %collective-permute-start.60 = (bf16[1,1,25,768]{3,2,1,0:T(8,128)(2,1)S(1)}, bf16[1,1,25,768]{3,2,1,0:T(8,128)(2,1)S(1)}, u32[]{:S(2)}, u32[]{:S(2)}) collective-permute-start(bf16[1,1,25,768]{3,2,1,0:T(8,128)(2,1)S(1)} %get-tuple-element.129), channel_id=1, source_target_pairs={{0,14},{1,15},{2,0},{3,1},{4,2},{5,3},{6,4},{7,5},{8,6},{9,7},{10,... | collective-permute-start | bytes 115208 | tf_op jit(solution)/shard_map/ppermute | solution.py:156
  508.3 62.7 %collective-permute-start.59 = (bf16[1,1,25,768]{3,2,1,0:T(8,128)(2,1)S(1)}, bf16[1,1,25,768]{3,2,1,0:T(8,128)(2,1)S(1)}, u32[]{:S(2)}, u32[]{:S(2)}) collective-permute-start(bf16[1,1,25,768]{3,2,1,0:T(8,128)(2,1)S(1)} %get-tuple-element.130), channel_id=1, source_target_pairs={{0,13},{1,14},{2,15},{3,0},{4,1},{5,2},{6,3},{7,4},{8,5},{9,6},{10... | collective-permute-start | bytes 115208 | tf_op jit(solution)/shard_map/ppermute | solution.py:156
  508.3 62.7 %collective-permute-start.58 = (bf16[1,1,25,768]{3,2,1,0:T(8,128)(2,1)S(1)}, bf16[1,1,25,768]{3,2,1,0:T(8,128)(2,1)S(1)}, u32[]{:S(2)}, u32[]{:S(2)}) collective-permute-start(bf16[1,1,25,768]{3,2,1,0:T(8,128)(2,1)S(1)} %get-tuple-element.131), channel_id=1, source_target_pairs={{0,12},{1,13},{2,14},{3,15},{4,0},{5,1},{6,2},{7,3},{8,4},{9,5},{1... | collective-permute-start | bytes 115208 | tf_op jit(solution)/shard_map/ppermute | solution.py:156
  510.0 6.8 collective-permute-start.48
  516.8 7.0 collective-permute-start.49
  529.7 6.8 collective-permute-start.51
  578.5 19.6 %all-to-all-start.3 = ((bf16[16,25,768]{2,1,0:T(8,128)(2,1)}), bf16[16,25,768]{2,1,0:T(8,128)(2,1)}, u32[]{:S(2)}, u32[]{:S(2)}) async-start(bf16[16,25,768]{2,1,0:T(8,128)(2,1)} %fusion.95), calls=%async_computation.3 | async-start | bytes 1572864 | tf_op jit(solution)/shard_map/all_to_all | solution.py:162
  646.8 8.1 collective-permute-start.63
  648.4 66.7 %collective-permute-start.77 = (bf16[1,1,25,768]{3,2,1,0:T(8,128)(2,1)S(1)}, bf16[1,1,25,768]{3,2,1,0:T(8,128)(2,1)S(1)}, u32[]{:S(2)}, u32[]{:S(2)}) collective-permute-start(bf16[1,1,25,768]{3,2,1,0:T(8,128)(2,1)S(1)} %get-tuple-element.113), channel_id=1, source_target_pairs={{0,15},{1,0},{2,1},{3,2},{4,3},{5,4},{6,5},{7,6},{8,7},{9,8},{10,9... | collective-permute-start | bytes 115208 | tf_op jit(solution)/shard_map/ppermute | solution.py:156
  652.5 62.5 %collective-permute-start.76 = (bf16[1,1,25,768]{3,2,1,0:T(8,128)(2,1)S(1)}, bf16[1,1,25,768]{3,2,1,0:T(8,128)(2,1)S(1)}, u32[]{:S(2)}, u32[]{:S(2)}) collective-permute-start(bf16[1,1,25,768]{3,2,1,0:T(8,128)(2,1)S(1)} %get-tuple-element.114), channel_id=1, source_target_pairs={{0,14},{1,15},{2,0},{3,1},{4,2},{5,3},{6,4},{7,5},{8,6},{9,7},{10,... | collective-permute-start | bytes 115208 | tf_op jit(solution)/shard_map/ppermute | solution.py:156
  653.2 61.8 %collective-permute-start.75 = (bf16[1,1,25,768]{3,2,1,0:T(8,128)(2,1)S(1)}, bf16[1,1,25,768]{3,2,1,0:T(8,128)(2,1)S(1)}, u32[]{:S(2)}, u32[]{:S(2)}) collective-permute-start(bf16[1,1,25,768]{3,2,1,0:T(8,128)(2,1)S(1)} %get-tuple-element.115), channel_id=1, source_target_pairs={{0,13},{1,14},{2,15},{3,0},{4,1},{5,2},{6,3},{7,4},{8,5},{9,6},{10... | collective-permute-start | bytes 115208 | tf_op jit(solution)/shard_map/ppermute | solution.py:156
  653.2 61.7 %collective-permute-start.74 = (bf16[1,1,25,768]{3,2,1,0:T(8,128)(2,1)S(1)}, bf16[1,1,25,768]{3,2,1,0:T(8,128)(2,1)S(1)}, u32[]{:S(2)}, u32[]{:S(2)}) collective-permute-start(bf16[1,1,25,768]{3,2,1,0:T(8,128)(2,1)S(1)} %get-tuple-element.116), channel_id=1, source_target_pairs={{0,12},{1,13},{2,14},{3,15},{4,0},{5,1},{6,2},{7,3},{8,4},{9,5},{1... | collective-permute-start | bytes 115208 | tf_op jit(solution)/shard_map/ppermute | solution.py:156
  655.0 6.8 collective-permute-start.64
  661.7 6.8 collective-permute-start.65
  674.4 6.8 collective-permute-start.67
  795.2 7.7 collective-permute-start.79
  795.9 67.3 %collective-permute-start.93 = (bf16[1,1,25,768]{3,2,1,0:T(8,128)(2,1)S(1)}, bf16[1,1,25,768]{3,2,1,0:T(8,128)(2,1)S(1)}, u32[]{:S(2)}, u32[]{:S(2)}) collective-permute-start(bf16[1,1,25,768]{3,2,1,0:T(8,128)(2,1)S(1)} %get-tuple-element.98), channel_id=1, source_target_pairs={{0,15},{1,0},{2,1},{3,2},{4,3},{5,4},{6,5},{7,6},{8,7},{9,8},{10,9... | collective-permute-start | bytes 115208 | tf_op jit(solution)/shard_map/ppermute | solution.py:156
  800.9 62.2 %collective-permute-start.92 = (bf16[1,1,25,768]{3,2,1,0:T(8,128)(2,1)S(1)}, bf16[1,1,25,768]{3,2,1,0:T(8,128)(2,1)S(1)}, u32[]{:S(2)}, u32[]{:S(2)}) collective-permute-start(bf16[1,1,25,768]{3,2,1,0:T(8,128)(2,1)S(1)} %get-tuple-element.99), channel_id=1, source_target_pairs={{0,14},{1,15},{2,0},{3,1},{4,2},{5,3},{6,4},{7,5},{8,6},{9,7},{10,... | collective-permute-start | bytes 115208 | tf_op jit(solution)/shard_map/ppermute | solution.py:156
  800.9 62.2 %collective-permute-start.91 = (bf16[1,1,25,768]{3,2,1,0:T(8,128)(2,1)S(1)}, bf16[1,1,25,768]{3,2,1,0:T(8,128)(2,1)S(1)}, u32[]{:S(2)}, u32[]{:S(2)}) collective-permute-start(bf16[1,1,25,768]{3,2,1,0:T(8,128)(2,1)S(1)} %get-tuple-element.100), channel_id=1, source_target_pairs={{0,13},{1,14},{2,15},{3,0},{4,1},{5,2},{6,3},{7,4},{8,5},{9,6},{10... | collective-permute-start | bytes 115208 | tf_op jit(solution)/shard_map/ppermute | solution.py:156
  800.9 62.2 %collective-permute-start.90 = (bf16[1,1,25,768]{3,2,1,0:T(8,128)(2,1)S(1)}, bf16[1,1,25,768]{3,2,1,0:T(8,128)(2,1)S(1)}, u32[]{:S(2)}, u32[]{:S(2)}) collective-permute-start(bf16[1,1,25,768]{3,2,1,0:T(8,128)(2,1)S(1)} %get-tuple-element.101), channel_id=1, source_target_pairs={{0,12},{1,13},{2,14},{3,15},{4,0},{5,1},{6,2},{7,3},{8,4},{9,5},{1... | collective-permute-start | bytes 115208 | tf_op jit(solution)/shard_map/ppermute | solution.py:156
  803.0 6.8 collective-permute-start.80
  809.8 6.8 collective-permute-start.81
  822.4 7.2 collective-permute-start.83
  829.7 6.5 collective-permute-start.84
  870.6 19.3 %all-to-all-start.5 = ((bf16[16,25,768]{2,1,0:T(8,128)(2,1)}), bf16[16,25,768]{2,1,0:T(8,128)(2,1)S(1)}, u32[]{:S(2)}, u32[]{:S(2)}) async-start(bf16[16,25,768]{2,1,0:T(8,128)(2,1)} %fusion.101), calls=%async_computation.5 | async-start | bytes 1572864 | tf_op jit(solution)/shard_map/all_to_all | solution.py:162
  876.9 82.9 %reduce-scatter.8.cloned.1.call-start = ((), (), s32[]{:S(2)}) async-start(), calls=%async_computation.12 | async-start | bytes 1769472 | tf_op jit(solution)/shard_map/reduce_scatter | solution.py:367
  911.4 71.6 %reduce-scatter.6.cloned.1.call-start = ((), (), s32[]{:S(2)}) async-start(), calls=%async_computation.11 | async-start | bytes 5308416 | tf_op jit(solution)/shard_map/reduce_scatter | solution.py:367
  931.3 67.6 %reduce-scatter.10.cloned.1.call-start = ((), (), s32[]{:S(2)}) async-start(), calls=%async_computation.13 | async-start | bytes 294912
  951.7 157.2 %all-reduce.10.cloned.1.call-start = ((), (), s32[]{:S(2)}) async-start(), calls=%async_computation.14 | async-start | bytes 4718592 | tf_op jit(solution)/shard_map/psum | solution.py:370
  (196 other events, 2924.9 us)
Sparse Core Ops, SparseCore 0:
  9.5 52.1 all-gather.2
  63.2 22.7 all-gather.4
  911.5 20.9 reduce-scatter.7
  935.2 47.7 reduce-scatter.5
  985.0 11.0 reduce-scatter.9
  999.5 109.2 all-reduce.9
